TPU v7x, 32 devices: a whole 2x2x4 slice. The times are simulated.
32 devices in a mesh: dp: 2 (over x), segment: 4 (over y, core), space: 4 (over z).
Axes of the slice: x: 2, y: 2, z: 4, core: 2. Of those that a mesh axis runs over, the one named last changes fastest.
Arguments:
- features: bfloat16 [2, 4, 32, 24, 6, 256], P('dp', 'segment', None, 'space'), may hold values from -6 to 6
- out_grad: bfloat16 [2, 4, 64, 12, 3, 128], P('dp', 'segment', None, 'space'), may hold values from -6 to 6
- weight_mean: float32 [4, 27, 2048], P('segment'), may hold values from -0.21875 to 0.21875
- weight_noise: float32 [4, 27, 2048], P('segment'), may hold values from -4 to 4
- precision: float32 [4, 27, 2048], P('segment'), may hold values from 0.5 to 4
Outputs:
- act_in: bfloat16 [2, 4, 64, 12, 3, 128], P('dp', 'segment', None, 'space')
- grad_in: bfloat16 [2, 4, 32, 24, 6, 256], P('dp', 'segment', None, 'space')
- mean_next: float32 [4, 27, 2048], P('segment')
- precision_next: float32 [4, 27, 2048], P('segment')
All inputs are finite; a program needn't handle non-finite values.
Results may differ from a plain program's by a relative error of at most 0.007.
Values may be sent and summed in bfloat16 or wider, within the bound.
No kernel may reach another device: no remote copies, remote signals or barrier semaphores. Data moves between devices by JAX's collectives and lax.ppermute only.
A program may use at most 64 MiB of HBM per device.

v0:
```python
import math
import jax
import jax.numpy as jnp
from jax import lax
from jax.sharding import PartitionSpec as P

CONV_LAYOUT = ("NCDHW", "OIDHW", "NCDHW")


def passed_along(block, axis, distance):
    devices = range(lax.axis_size(axis))
    route = [(i - distance, i) for i in devices if i - distance in devices]
    return lax.ppermute(block, axis, route)


def noisy_weights(weight_mean, weight_noise, precision, cout, cin):
    noisy = weight_mean + weight_noise * lax.rsqrt(2000.0 * (precision + 0.1))
    kernel = noisy.astype(jnp.bfloat16).reshape(3, 3, 3, cout, cin)
    return jnp.transpose(kernel, (3, 4, 0, 1, 2))


def forward_conv(padded, kernel):
    return lax.conv_general_dilated(
        padded[None],
        kernel,
        (2, 2, 2),
        "VALID",
        dimension_numbers=CONV_LAYOUT,
        preferred_element_type=jnp.float32,
    )[0]


def input_conv(pre_grad, kernel):
    flipped = jnp.transpose(kernel[:, :, ::-1, ::-1, ::-1], (1, 0, 2, 3, 4))
    return lax.conv_general_dilated(
        pre_grad[None],
        flipped,
        (1, 1, 1),
        ((2, 2), (2, 2), (2, 2)),
        lhs_dilation=(2, 2, 2),
        dimension_numbers=CONV_LAYOUT,
        preferred_element_type=jnp.float32,
    )[0]


def weight_conv(padded, pre_grad):
    grads = lax.conv_general_dilated(
        padded[:, None],
        pre_grad[:, None],
        (1, 1, 1),
        "VALID",
        rhs_dilation=(2, 2, 2),
        dimension_numbers=CONV_LAYOUT,
        preferred_element_type=jnp.float32,
    )
    return jnp.transpose(grads, (2, 3, 4, 1, 0)).reshape(27, -1)


def input_grad(pre_grad, kernel):
    spread_grad = input_conv(pre_grad, kernel)
    rim_plane = passed_along(spread_grad[:, 0, 1:, 1:], "space", -1)
    interior = spread_grad[:, 1:, 1:, 1:]
    interior = jnp.concatenate([interior[:, :-1], interior[:, -1:] + rim_plane[:, None]], axis=1)
    return interior.astype(jnp.bfloat16)


def per_device(features, out_grad, weight_mean, weight_noise, precision):
    feats = features[0, 0]
    grads = out_grad[0, 0]
    mean = weight_mean[0]
    prec = precision[0]
    cin = feats.shape[0]
    cout = grads.shape[0]
    kernel = noisy_weights(mean, weight_noise[0], prec, cout, cin)
    below = passed_along(feats[:, -1:], "space", 1)
    padded = jnp.pad(jnp.concatenate([below, feats], axis=1), ((0, 0), (0, 0), (1, 0), (1, 0)))
    preact = forward_conv(padded, kernel)
    activation = jax.nn.silu(preact).astype(jnp.bfloat16)
    act_in = passed_along(activation, "segment", 1)
    squash = jax.nn.sigmoid(preact)
    pre_grad = (grads.astype(jnp.float32) * squash * (1.0 + preact * (1.0 - squash))).astype(
        jnp.bfloat16
    )
    grad_in = passed_along(input_grad(pre_grad, kernel), "segment", -1)
    local_grad = weight_conv(padded, pre_grad)
    cell_count = (
        lax.axis_size("dp")
        * lax.axis_size("space")
        * pre_grad.shape[1]
        * pre_grad.shape[2]
        * pre_grad.shape[3]
    )
    inv_root = 1.0 / math.sqrt(cell_count)
    grad_total = lax.psum(local_grad.astype(jnp.bfloat16), ("dp", "space")).astype(jnp.float32)
    scaled = grad_total * inv_root
    prec_next = 0.75 * prec + 0.25 * scaled * scaled
    mean_new = mean - 0.03 * scaled / (prec_next + 0.1)
    return (act_in[None, None], grad_in[None, None], mean_new[None], prec_next[None])


def solution(mesh):
    in_specs = (
        P("dp", "segment", None, "space", None, None),
        P("dp", "segment", None, "space", None, None),
        P("segment", None, None),
        P("segment", None, None),
        P("segment", None, None),
    )
    out_specs = (
        P("dp", "segment", None, "space", None, None),
        P("dp", "segment", None, "space", None, None),
        P("segment", None, None),
        P("segment", None, None),
    )
    return jax.shard_map(
        per_device, mesh=mesh, in_specs=in_specs, out_specs=out_specs, check_vma=False
    )
```

profile of v0, /device:TPU:0, one launch (start us, length us, event | category | flops | bytes accessed | tf_op | source)
XLA Modules:
  0.0 176.4 jit_solution(7315777036722529213)
XLA Ops:
  7.2 0.9 slice.26
  8.1 4.9 %collective-permute-start = (bf16[32,1,6,256]{3,0,2,1:T(8,128)(2,1)S(1)}, bf16[32,1,6,256]{3,0,2,1:T(8,128)(2,1)S(1)}, u32[]{:S(2)}, u32[]{:S(2)}) collective-permute-start(bf16[32,1,6,256]{3,0,2,1:T(8,128)(2,1)S(1)} %slice.26), channel_id=1, source_target_pairs={{0,1},{1,2},{2,3},{4,5},{5,6},{6,7},{8,9},{9,10},{10,11},{12,13},{... | collective-permute-start | bytes 294920 | tf_op jit(solution)/shard_map/ppermute | solution.py:13
  13.1 2.0 %convert_reduce_fusion = bf16[27,2048]{1,0:T(8,128)(2,1)S(1)} fusion(f32[1,27,2048]{2,0,1:T(1,128)} %param.7, f32[1,27,2048]{2,0,1:T(1,128)} %param.8, f32[1,27,2048]{2,0,1:T(1,128)} %param.9), kind=kLoop, calls=%fused_computation.61 | loop fusion | flops 276480 | bytes 774144 | tf_op jit(solution)/shard_map/convert_element_type | solution.py:18
  15.1 1.1 reshape.121
  16.2 2.6 %fusion.55 = (bf16[32,1,7,7,257]{4,0,3,2,1:T(8,128)(2,1)}, bf16[32,7,7,1,257]{4,0,2,1,3:T(8,128)(2,1)S(1)}) fusion(bf16[32,6,6,256]{3,0,2,1:T(8,128)(2,1)} %bitcast.115, bf16[32,1,6,256]{3,0,2,1:T(8,128)(2,1)S(1)} %collective-permute-done), kind=kLoop, calls=%fused_computation.75 | loop fusion | flops 4432736 | bytes 2300032 | tf_op jit(solution)/shard_map/broadcast_in_dim | solution.py:48
  18.8 1.2 pad.5
  20.0 4.4 %reshape.91 = bf16[32,7,7,1,8,34]{5,4,0,2,1,3:T(8,128)(2,1)S(1)} reshape(bf16[32,7,7,1,272]{4,0,2,1,3:T(8,128)(2,1)} %pad.5) | data formatting | bytes 1705984 | tf_op jit(solution)/shard_map/conv_general_dilated | solution.py:23
  24.4 5.3 %copy.29 = bf16[32,7,7,1,8,34]{0,4,5,2,1,3:T(8,128)(2,1)} copy(bf16[32,7,7,1,8,34]{5,4,0,2,1,3:T(8,128)(2,1)S(1)} %reshape.91) | data formatting | bytes 1705984 | tf_op jit(solution)/shard_map/conv_general_dilated | solution.py:23
  29.6 1.0 slice.27
  30.6 4.3 %add_divide_fusion = (f32[3,3,8,17,64]{4,2,3,1,0:T(8,128)S(1)}, f32[3,3,8,17,64]{4,2,3,1,0:T(8,128)S(1)}, f32[3,3,8,17,64]{4,2,3,1,0:T(8,128)S(1)}) fusion(bf16[3,3,3,64,32]{4,3,2,1,0:T(8,128)(2,1)} %reshape.121, bf16[32,7,7,1,7,2]{0,4,5,2,1,3:T(8,128)(2,1)S(1)} %slice.27, bf16[32,7,7,1,8,34]{0,4,5,2,1,3:T(8,128)(2,1)} %copy.29, pred[8,17]{0,1:T(8,128)(4,1)S(1)} %copy-done.8), kind=kOutput, calls=%fused_computation.25 | convolution fusion | flops 138622464 | bytes 1947656 | tf_op jit(solution)/shard_map/conv_general_dilated | solution.py:23
  34.9 0.1 copy.32
  35.0 0.1 reshape.104
  35.2 0.2 copy.48
  35.4 0.1 copy.34
  35.5 0.1 reshape.106
  35.6 0.2 copy.49
  35.9 0.4 copy-done.6
  36.3 0.1 fusion.46
  36.4 0.2 copy.50
  36.6 0.1 pad.7.clone
  36.7 0.1 reshape.98
  36.9 0.1 copy.30
  37.0 0.1 reshape.95
  37.1 0.2 copy.47
  37.4 0.1 fusion.30
  37.5 1.7 copy.41
  39.2 13.4 %copy.40 = bf16[32,1,7,7,257]{0,1,4,3,2:T(2,128)(2,1)} copy(bf16[32,1,7,7,257]{4,0,3,2,1:T(8,128)(2,1)S(1)} %copy-done) | data formatting | bytes 1611904 | tf_op jit(solution)/shard_map/broadcast_in_dim | solution.py:48
  52.6 6.5 %broadcast_select_fusion = f32[7,7,8,34,32]{4,2,3,1,0:T(8,128)} fusion(pred[8,34]{0,1:T(8,128)(4,1)S(1)} %copy-done.7, bf16[3,3,3,64,32]{4,3,2,1,0:T(8,128)(2,1)S(1)} %copy-done.2, bf16[64,3,3,1,7,1]{0,4,5,2,1,3:T(8,128)(2,1)S(1)} %slice.31, bf16[64,3,3,1,8,17]{0,4,5,2,1,3:T(8,128)(2,1)S(1)} %copy.38), kind=kOutput, calls=%fused_computation.8 | convolution fusion | flops 136288768 | bytes 1981584 | tf_op jit(solution)/shard_map/conv_general_dilated | solution.py:35
  59.1 9.5 %copy.39 = f32[7,7,8,34,32]{3,2,4,1,0:T(8,128)} copy(f32[7,7,8,34,32]{4,2,3,1,0:T(8,128)} %broadcast_select_fusion) | data formatting | bytes 3411968 | tf_op jit(solution)/shard_map/conv_general_dilated | solution.py:35
  68.6 4.9 %reshape.102 = f32[7,7,1,272,32]{3,4,1,0,2:T(8,128)S(1)} reshape(f32[7,7,8,34,32]{3,2,4,1,0:T(8,128)} %copy.39) | data formatting | bytes 3411968 | tf_op jit(solution)/shard_map/conv_general_dilated | solution.py:35
  73.5 0.2 slice_bitcast_fusion
  73.7 0.1 slice_bitcast_fusion.1
  73.8 1.3 collective-permute-start.2
  75.1 15.4 %convolution_convert_fusion = bf16[3,3,3,64,32]{3,4,2,1,0:T(8,128)(2,1)S(1)} fusion(bf16[32,1,7,7,257]{0,1,4,3,2:T(2,128)(2,1)} %copy.40, bf16[64,1,3,3,128]{0,1,4,3,2:T(2,128)(2,1)S(1)} %copy-done.5), kind=kOutput, calls=%fused_computation.19 | convolution fusion | flops 127457280 | bytes 1064000 | tf_op jit(solution)/shard_map/transpose | solution.py:56
  90.6 0.2 slice.42
  90.8 0.3 copy.42
  91.0 1.2 convert_element_type.66
  92.2 1.1 fusion.44
  93.3 0.1 pad_maximum_fusion
  93.4 1.3 collective-permute-start.3
  94.7 0.1 fusion.38
  94.8 3.0 %collective-permute-start.1 = (bf16[64,3,3,128]{3,0,2,1:T(8,128)(2,1)S(1)}, bf16[64,3,3,128]{3,0,2,1:T(8,128)(2,1)S(1)}, u32[]{:S(2)}, u32[]{:S(2)}) collective-permute-start(bf16[64,3,3,128]{3,0,2,1:T(8,128)(2,1)S(1)} %fusion.38), channel_id=1, source_target_pairs={{0,4},{4,8},{8,12},{1,5},{5,9},{9,13},{2,6},{6,10},{10,14},{3,7},{... | collective-permute-start | bytes 442376 | tf_op jit(solution)/shard_map/ppermute | solution.py:13
  97.8 67.3 %all-reduce.3.cloned.1.call-done = bf16[27,2048]{1,0:T(8,128)(2,1)} async-done(((bf16[27,2048]{1,0:T(8,128)(2,1)}), bf16[27,2048]{1,0:T(8,128)(2,1)}) %all-reduce.3.cloned.1.call-update) | async-done | bytes 110608 | tf_op jit(solution)/shard_map/psum | solution.py:94
  165.2 1.1 fusion.47
  166.3 0.9 copy.45
  167.2 0.9 copy.44
  168.1 0.7 copy.62
  168.8 0.8 copy.63
  (28 shorter events, 0.3 us)
Async XLA Ops:
  7.2 158.0 %all-reduce.3.cloned.1.call-start = ((), (), s32[]{:S(2)}) async-start(), calls=%async_computation | async-start | bytes 262144 | tf_op jit(solution)/shard_map/psum | solution.py:94
  8.1 8.1 %collective-permute-start = (bf16[32,1,6,256]{3,0,2,1:T(8,128)(2,1)S(1)}, bf16[32,1,6,256]{3,0,2,1:T(8,128)(2,1)S(1)}, u32[]{:S(2)}, u32[]{:S(2)}) collective-permute-start(bf16[32,1,6,256]{3,0,2,1:T(8,128)(2,1)S(1)} %slice.26), channel_id=1, source_target_pairs={{0,1},{1,2},{2,3},{4,5},{5,6},{6,7},{8,9},{9,10},{10,11},{12,13},{... | collective-permute-start | bytes 294920 | tf_op jit(solution)/shard_map/ppermute | solution.py:13
  24.3 6.3 %copy-start.8 = (pred[8,17]{0,1:T(8,128)(4,1)S(1)}, pred[8,17]{0,1:T(8,128)(4,1)}, u32[]{:S(2)}) copy-start(pred[8,17]{0,1:T(8,128)(4,1)} %constant.36) | copy-start | bytes 412
  35.4 0.9 copy-start.6
  37.0 2.2 %copy-start = (bf16[32,1,7,7,257]{4,0,3,2,1:T(8,128)(2,1)S(1)}, bf16[32,1,7,7,257]{4,0,3,2,1:T(8,128)(2,1)}, u32[]{:S(2)}) copy-start(bf16[32,1,7,7,257]{4,0,3,2,1:T(8,128)(2,1)} %get-tuple-element.12) | copy-start | bytes 2417860
  39.2 13.4 %copy-start.2 = (bf16[3,3,3,64,32]{4,3,2,1,0:T(8,128)(2,1)S(1)}, bf16[3,3,3,64,32]{4,3,2,1,0:T(8,128)(2,1)}, u32[]{:S(2)}) copy-start(bf16[3,3,3,64,32]{4,3,2,1,0:T(8,128)(2,1)} %reshape.121) | copy-start | bytes 331780
  39.2 13.4 %copy-start.7 = (pred[8,34]{0,1:T(8,128)(4,1)S(1)}, pred[8,34]{0,1:T(8,128)(4,1)}, u32[]{:S(2)}) copy-start(pred[8,34]{0,1:T(8,128)(4,1)} %constant.37) | copy-start | bytes 820
  73.5 1.6 copy-start.5
  73.7 16.8 %copy-start.1 = (f32[32,7,7,257]{3,0,2,1:T(8,128)}, f32[32,7,7,257]{3,0,2,1:T(8,128)S(1)}, u32[]{:S(2)}) copy-start(f32[32,7,7,257]{3,0,2,1:T(8,128)S(1)} %slice_bitcast_fusion) | copy-start | bytes 4835716
  73.8 18.4 %collective-permute-start.2 = (f32[32,6,256]{2,0,1:T(8,128)S(1)}, f32[32,6,256]{2,0,1:T(8,128)S(1)}, u32[]{:S(2)}, u32[]{:S(2)}) collective-permute-start(f32[32,6,256]{2,0,1:T(8,128)S(1)} %slice_bitcast_fusion.1), channel_id=1, source_target_pairs={{1,0},{2,1},{3,2},{5,4},{6,5},{7,6},{9,8},{10,9},{11,10},{13,12},{... | collective-permute-start | bytes 589832 | tf_op jit(solution)/shard_map/ppermute | solution.py:13
  90.5 74.6 %copy-start.3 = (f32[1,27,2048]{2,0,1:T(1,128)S(1)}, f32[1,27,2048]{2,0,1:T(1,128)}, u32[]{:S(2)}) copy-start(f32[1,27,2048]{2,0,1:T(1,128)} %param.7) | copy-start | bytes 663556
  90.5 74.6 %copy-start.4 = (f32[1,27,2048]{2,0,1:T(1,128)S(1)}, f32[1,27,2048]{2,0,1:T(1,128)}, u32[]{:S(2)}) copy-start(f32[1,27,2048]{2,0,1:T(1,128)} %param.9) | copy-start | bytes 663556
  93.4 74.7 %collective-permute-start.3 = (bf16[32,6,6,256]{3,0,2,1:T(8,128)(2,1)S(1)}, bf16[32,6,6,256]{3,0,2,1:T(8,128)(2,1)S(1)}, u32[]{:S(2)}, u32[]{:S(2)}) collective-permute-start(bf16[32,6,6,256]{3,0,2,1:T(8,128)(2,1)S(1)} %pad_maximum_fusion), channel_id=1, source_target_pairs={{4,0},{8,4},{12,8},{5,1},{9,5},{13,9},{6,2},{10,6},{14,10},{7,3},{... | collective-permute-start | bytes 1769480 | tf_op jit(solution)/shard_map/ppermute | solution.py:13
  94.8 73.3 %collective-permute-start.1 = (bf16[64,3,3,128]{3,0,2,1:T(8,128)(2,1)S(1)}, bf16[64,3,3,128]{3,0,2,1:T(8,128)(2,1)S(1)}, u32[]{:S(2)}, u32[]{:S(2)}) collective-permute-start(bf16[64,3,3,128]{3,0,2,1:T(8,128)(2,1)S(1)} %fusion.38), channel_id=1, source_target_pairs={{0,4},{4,8},{8,12},{1,5},{5,9},{9,13},{2,6},{6,10},{10,14},{3,7},{... | collective-permute-start | bytes 442376 | tf_op jit(solution)/shard_map/ppermute | solution.py:13
Sparse Core Ops, SparseCore 0:
  92.3 72.7 all-reduce.2
where the time goes:
time: 177 us; the launch traced here: 176 us
  waiting for transfers between devices  67.4 us (38%)
  local copies, waits for them, and re-layouts  50.8 us (29%)
  matrix products  26.1 us (15%)
  between operations  14.3 us (8%)
  starting transfers between devices  10.6 us (6%)
  other arithmetic  7.14 us (4%)
    psum x1, waiting for transfers between devices, per_device(): lax.psum(local_grad.astype(jnp.bfloat16), ('dp', 'space'))  67.3 us
    transpose x1, matrix products, weight_conv(): return jnp.transpose(grads, (2, 3, 4, 1, 0)).reshape(27, -1)  15.4 us
    conv_general_dilated x5, local copies, waits for them, and re-layouts, input_conv(): lax.conv_general_dilated(pre_grad[None], flipped, (1, 1, 1), ((2, 2), (2,...  14.6 us
    broadcast_in_dim x1, local copies, waits for them, and re-layouts, weight_conv(): padded[:, None]  13.4 us
    conv_general_dilated x6, local copies, waits for them, and re-layouts, forward_conv(): lax.conv_general_dilated(padded[None], kernel, (2, 2, 2), 'VALID', dimens...  10.8 us
    ppermute x4, starting transfers between devices, passed_along(): return lax.ppermute(block, axis, route)  10.6 us
    conv_general_dilated x1, matrix products, input_conv(): lax.conv_general_dilated(pre_grad[None], flipped, (1, 1, 1), ((2, 2), (2,...  6.48 us
    unnamed x26, local copies, waits for them, and re-layouts  4.65 us
  transfers between devices with their start and end apart: 5, of which 1 were waited for; matrix products, arithmetic and copies ran while one was open for 14% of the time, Pallas kernels for 0%

commit v1 on v0

--- a/solution.py
+++ b/solution.py
@@ -91,7 +91,9 @@
         * pre_grad.shape[3]
     )
     inv_root = 1.0 / math.sqrt(cell_count)
-    grad_total = lax.psum(local_grad.astype(jnp.bfloat16), ("dp", "space")).astype(jnp.float32)
+    grad_total = jnp.sum(
+        lax.all_gather(local_grad.astype(jnp.bfloat16), ("dp", "space")), axis=0
+    ).astype(jnp.float32)
     scaled = grad_total * inv_root
     prec_next = 0.75 * prec + 0.25 * scaled * scaled
     mean_new = mean - 0.03 * scaled / (prec_next + 0.1)

time: 177 us -> 140 us (0.79)
  the two profiles are of different devices: /device:TPU:0 before, /device:TPU:1 now
where the time goes in v1:
time: 140 us; the launch traced here: 139 us
  local copies, waits for them, and re-layouts  48.6 us (35%)
  blocking collectives  34.6 us (25%)
  matrix products  25.9 us (18%)
  starting transfers between devices  14 us (10%)
  other arithmetic  7.62 us (5%)
  waiting for transfers between devices  7.32 us (5%)
    all_gather x1, blocking collectives, per_device(): lax.all_gather(local_grad.astype(jnp.bfloat16), ('dp', 'space'))  34.6 us
    transpose x1, matrix products, weight_conv(): return jnp.transpose(grads, (2, 3, 4, 1, 0)).reshape(27, -1)  15.2 us
    conv_general_dilated x5, local copies, waits for them, and re-layouts, input_conv(): lax.conv_general_dilated(pre_grad[None], flipped, (1, 1, 1), ((2, 2), (2,...  14.6 us
    ppermute x4, starting transfers between devices, passed_along(): return lax.ppermute(block, axis, route)  14 us
    broadcast_in_dim x1, local copies, waits for them, and re-layouts, weight_conv(): padded[:, None]  13.4 us
    conv_general_dilated x6, local copies, waits for them, and re-layouts, forward_conv(): lax.conv_general_dilated(padded[None], kernel, (2, 2, 2), 'VALID', dimens...  10.9 us
    ppermute x4, waiting for transfers between devices, passed_along(): return lax.ppermute(block, axis, route)  7.32 us
    conv_general_dilated x1, matrix products, input_conv(): lax.conv_general_dilated(pre_grad[None], flipped, (1, 1, 1), ((2, 2), (2,...  6.48 us
  transfers between devices with their start and end apart: 4, of which 1 were waited for; matrix products, arithmetic and copies ran while one was open for 26% of the time, Pallas kernels for 0%

profile of v1, /device:TPU:1, one launch (start us, length us, event | category | flops | bytes accessed | tf_op | source)
XLA Modules:
  0.0 139.1 jit_solution(3146580076960529497)
XLA Ops:
  0.6 0.9 slice.26
  1.5 4.0 %collective-permute-start = (bf16[32,1,6,256]{3,0,2,1:T(8,128)(2,1)S(1)}, bf16[32,1,6,256]{3,0,2,1:T(8,128)(2,1)S(1)}, u32[]{:S(2)}, u32[]{:S(2)}) collective-permute-start(bf16[32,1,6,256]{3,0,2,1:T(8,128)(2,1)S(1)} %slice.26), channel_id=1, source_target_pairs={{0,1},{1,2},{2,3},{4,5},{5,6},{6,7},{8,9},{9,10},{10,11},{12,13},{... | collective-permute-start | bytes 294920 | tf_op jit(solution)/shard_map/ppermute | solution.py:13
  5.6 2.0 %convert_reduce_fusion = bf16[27,2048]{1,0:T(8,128)(2,1)S(1)} fusion(f32[1,27,2048]{2,0,1:T(1,128)} %param.7, f32[1,27,2048]{2,0,1:T(1,128)} %param.8, f32[1,27,2048]{2,0,1:T(1,128)} %param.9), kind=kLoop, calls=%fused_computation.58 | loop fusion | flops 276480 | bytes 774144 | tf_op jit(solution)/shard_map/convert_element_type | solution.py:18
  7.6 1.1 reshape.160
  8.6 2.6 %fusion.51 = (bf16[32,1,7,7,257]{4,0,3,2,1:T(8,128)(2,1)}, bf16[32,7,7,1,257]{4,0,2,1,3:T(8,128)(2,1)S(1)}) fusion(bf16[32,6,6,256]{3,0,2,1:T(8,128)(2,1)} %bitcast.105, bf16[32,1,6,256]{3,0,2,1:T(8,128)(2,1)S(1)} %collective-permute-done), kind=kLoop, calls=%fused_computation.72 | loop fusion | flops 4432736 | bytes 2300032 | tf_op jit(solution)/shard_map/broadcast_in_dim | solution.py:48
  11.2 1.2 pad.5
  12.4 4.4 %reshape.130 = bf16[32,7,7,1,8,34]{5,4,0,2,1,3:T(8,128)(2,1)S(1)} reshape(bf16[32,7,7,1,272]{4,0,2,1,3:T(8,128)(2,1)} %pad.5) | data formatting | bytes 1705984 | tf_op jit(solution)/shard_map/conv_general_dilated | solution.py:23
  16.8 5.3 %copy.41 = bf16[32,7,7,1,8,34]{0,4,5,2,1,3:T(8,128)(2,1)} copy(bf16[32,7,7,1,8,34]{5,4,0,2,1,3:T(8,128)(2,1)S(1)} %reshape.130) | data formatting | bytes 1705984 | tf_op jit(solution)/shard_map/conv_general_dilated | solution.py:23
  22.1 1.0 slice.27
  23.1 4.3 %add_divide_fusion = (f32[3,3,8,17,64]{4,2,3,1,0:T(8,128)S(1)}, f32[3,3,8,17,64]{4,2,3,1,0:T(8,128)S(1)}, f32[3,3,8,17,64]{4,2,3,1,0:T(8,128)S(1)}) fusion(bf16[3,3,3,64,32]{4,3,2,1,0:T(8,128)(2,1)} %reshape.160, bf16[32,7,7,1,7,2]{0,4,5,2,1,3:T(8,128)(2,1)S(1)} %slice.27, bf16[32,7,7,1,8,34]{0,4,5,2,1,3:T(8,128)(2,1)} %copy.41, pred[8,17]{0,1:T(8,128)(4,1)S(1)} %copy-done.7), kind=kOutput, calls=%fused_computation.25 | convolution fusion | flops 138622464 | bytes 1947656 | tf_op jit(solution)/shard_map/conv_general_dilated | solution.py:23
  27.3 0.1 copy.44
  27.5 0.1 reshape.143
  27.6 0.2 copy.57
  27.8 0.1 copy.46
  28.0 0.1 reshape.145
  28.1 0.2 copy.58
  28.3 0.1 copy.42
  28.6 0.2 copy.56
  28.8 0.1 fusion.38
  28.9 0.3 copy-done.5
  29.2 0.1 fusion.30
  29.3 0.1 fusion.43
  29.4 0.2 copy.59
  29.6 0.1 pad.7.clone
  29.7 0.1 reshape.137
  29.9 6.5 %broadcast_select_fusion = f32[7,7,8,34,32]{4,2,3,1,0:T(8,128)} fusion(pred[8,34]{0,1:T(8,128)(4,1)S(1)} %copy-done.6, bf16[3,3,3,64,32]{4,3,2,1,0:T(8,128)(2,1)S(1)} %copy-done.2, bf16[64,3,3,1,7,1]{0,4,5,2,1,3:T(8,128)(2,1)S(1)} %slice.31, bf16[64,3,3,1,8,17]{0,4,5,2,1,3:T(8,128)(2,1)S(1)} %copy.50), kind=kOutput, calls=%fused_computation.8 | convolution fusion | flops 136288768 | bytes 1981584 | tf_op jit(solution)/shard_map/conv_general_dilated | solution.py:35
  36.4 9.6 %copy.51 = f32[7,7,8,34,32]{3,2,4,1,0:T(8,128)} copy(f32[7,7,8,34,32]{4,2,3,1,0:T(8,128)} %broadcast_select_fusion) | data formatting | bytes 3411968 | tf_op jit(solution)/shard_map/conv_general_dilated | solution.py:35
  46.0 4.9 %reshape.141 = f32[7,7,1,272,32]{3,4,1,0,2:T(8,128)S(1)} reshape(f32[7,7,8,34,32]{3,2,4,1,0:T(8,128)} %copy.51) | data formatting | bytes 3411968 | tf_op jit(solution)/shard_map/conv_general_dilated | solution.py:35
  50.9 0.2 slice_bitcast_fusion
  51.1 0.1 slice_bitcast_fusion.1
  51.2 1.4 copy-done.1
  52.5 0.2 slice.42
  52.8 4.0 %collective-permute-start.1 = (bf16[64,3,3,128]{3,0,2,1:T(8,128)(2,1)S(1)}, bf16[64,3,3,128]{3,0,2,1:T(8,128)(2,1)S(1)}, u32[]{:S(2)}, u32[]{:S(2)}) collective-permute-start(bf16[64,3,3,128]{3,0,2,1:T(8,128)(2,1)S(1)} %fusion.38), channel_id=1, source_target_pairs={{0,4},{4,8},{8,12},{1,5},{5,9},{9,13},{2,6},{6,10},{10,14},{3,7},{... | collective-permute-start | bytes 442376 | tf_op jit(solution)/shard_map/ppermute | solution.py:13
  56.8 0.7 copy.53
  57.5 13.4 %copy.52 = bf16[32,1,7,7,257]{0,1,4,3,2:T(2,128)(2,1)} copy(bf16[32,1,7,7,257]{4,0,3,2,1:T(8,128)(2,1)S(1)} %copy-done) | data formatting | bytes 1611904 | tf_op jit(solution)/shard_map/broadcast_in_dim | solution.py:48
  70.9 15.2 %convolution_convert_fusion = bf16[3,3,3,64,32]{3,4,2,1,0:T(8,128)(2,1)S(1)} fusion(bf16[32,1,7,7,257]{0,1,4,3,2:T(2,128)(2,1)} %copy.52, bf16[64,1,3,3,128]{0,1,4,3,2:T(2,128)(2,1)S(1)} %copy.53), kind=kOutput, calls=%fused_computation.19 | convolution fusion | flops 127457280 | bytes 1064000 | tf_op jit(solution)/shard_map/transpose | solution.py:56
  86.1 0.3 copy.54
  86.4 0.5 convert_element_type.87
  86.9 1.4 %collective-permute-start.2 = (f32[32,6,256]{2,0,1:T(8,128)S(1)}, f32[32,6,256]{2,0,1:T(8,128)S(1)}, u32[]{:S(2)}, u32[]{:S(2)}) collective-permute-start(f32[32,6,256]{2,0,1:T(8,128)S(1)} %slice_bitcast_fusion.1), channel_id=1, source_target_pairs={{1,0},{2,1},{3,2},{5,4},{6,5},{7,6},{9,8},{10,9},{11,10},{13,12},{... | collective-permute-start | bytes 589832 | tf_op jit(solution)/shard_map/ppermute | solution.py:13
  88.3 34.6 %all_gather.4 = bf16[8,27,2048]{2,1,0:T(8,128)(2,1)S(1)} all-gather(bf16[1,27,2048]{2,1,0:T(8,128)(2,1)S(1)} %convert_element_type.87), channel_id=1, replica_groups=mesh['dp'=2,'segment'=4,'space'=4] {'dp','space'}, dimensions={0}, use_global_device_ids=true | all-gather | bytes 995328 | tf_op jit(solution)/shard_map/all_gather | solution.py:95
  122.9 0.2 reduce_sum.12
  123.1 1.1 fusion.41
  124.2 0.1 pad_maximum_fusion
  124.3 4.6 %collective-permute-start.3 = (bf16[32,6,6,256]{3,0,2,1:T(8,128)(2,1)S(1)}, bf16[32,6,6,256]{3,0,2,1:T(8,128)(2,1)S(1)}, u32[]{:S(2)}, u32[]{:S(2)}) collective-permute-start(bf16[32,6,6,256]{3,0,2,1:T(8,128)(2,1)S(1)} %pad_maximum_fusion), channel_id=1, source_target_pairs={{4,0},{8,4},{12,8},{5,1},{9,5},{13,9},{6,2},{10,6},{14,10},{7,3},{... | collective-permute-start | bytes 1769480 | tf_op jit(solution)/shard_map/ppermute | solution.py:13
  128.9 1.4 %divide_subtract_fusion = (f32[1,27,2048]{2,0,1:T(1,128)}, f32[1,27,2048]{2,0,1:T(1,128)}) fusion(f32[1,27,2048]{2,0,1:T(1,128)S(1)} %copy-done.3, f32[27,2048]{1,0:T(8,128)S(1)} %get-tuple-element.19, f32[1,27,2048]{2,1,0:T(8,128)S(1)} %get-tuple-element.18, f32[1,27,2048]{2,0,1:T(1,128)S(1)} %copy-done.4), kind=kLoop, calls=%fused_computation.59 | loop fusion | flops 276480 | bytes 1327104 | tf_op jit(solution)/shard_map/sub | solution.py:99
  130.3 7.3 %collective-permute-done.3 = bf16[32,6,6,256]{3,0,2,1:T(8,128)(2,1)S(1)} collective-permute-done((bf16[32,6,6,256]{3,0,2,1:T(8,128)(2,1)S(1)}, bf16[32,6,6,256]{3,0,2,1:T(8,128)(2,1)S(1)}, u32[]{:S(2)}, u32[]{:S(2)}) %collective-permute-start.3) | collective-permute-done | bytes 589856 | tf_op jit(solution)/shard_map/ppermute | solution.py:13
  137.7 0.7 copy.64
  138.3 0.8 copy.65
  (24 shorter events, 0.3 us)
Async XLA Ops:
  1.5 7.1 %collective-permute-start = (bf16[32,1,6,256]{3,0,2,1:T(8,128)(2,1)S(1)}, bf16[32,1,6,256]{3,0,2,1:T(8,128)(2,1)S(1)}, u32[]{:S(2)}, u32[]{:S(2)}) collective-permute-start(bf16[32,1,6,256]{3,0,2,1:T(8,128)(2,1)S(1)} %slice.26), channel_id=1, source_target_pairs={{0,1},{1,2},{2,3},{4,5},{5,6},{6,7},{8,9},{9,10},{10,11},{12,13},{... | collective-permute-start | bytes 294920 | tf_op jit(solution)/shard_map/ppermute | solution.py:13
  16.8 6.3 %copy-start.7 = (pred[8,17]{0,1:T(8,128)(4,1)S(1)}, pred[8,17]{0,1:T(8,128)(4,1)}, u32[]{:S(2)}) copy-start(pred[8,17]{0,1:T(8,128)(4,1)} %constant.38) | copy-start | bytes 412
  28.3 0.9 copy-start.5
  28.8 1.2 copy-start.2
  28.8 1.2 copy-start.6
  51.0 1.5 %copy-start.1 = (f32[32,7,7,257]{3,0,2,1:T(8,128)}, f32[32,7,7,257]{3,0,2,1:T(8,128)S(1)}, u32[]{:S(2)}) copy-start(f32[32,7,7,257]{3,0,2,1:T(8,128)S(1)} %slice_bitcast_fusion) | copy-start | bytes 4835716
  51.0 6.5 %copy-start = (bf16[32,1,7,7,257]{4,0,3,2,1:T(8,128)(2,1)S(1)}, bf16[32,1,7,7,257]{4,0,3,2,1:T(8,128)(2,1)}, u32[]{:S(2)}) copy-start(bf16[32,1,7,7,257]{4,0,3,2,1:T(8,128)(2,1)} %get-tuple-element.14) | copy-start | bytes 2417860
  52.8 77.6 %collective-permute-start.1 = (bf16[64,3,3,128]{3,0,2,1:T(8,128)(2,1)S(1)}, bf16[64,3,3,128]{3,0,2,1:T(8,128)(2,1)S(1)}, u32[]{:S(2)}, u32[]{:S(2)}) collective-permute-start(bf16[64,3,3,128]{3,0,2,1:T(8,128)(2,1)S(1)} %fusion.38), channel_id=1, source_target_pairs={{0,4},{4,8},{8,12},{1,5},{5,9},{9,13},{2,6},{6,10},{10,14},{3,7},{... | collective-permute-start | bytes 442376 | tf_op jit(solution)/shard_map/ppermute | solution.py:13
  86.8 42.1 %copy-start.3 = (f32[1,27,2048]{2,0,1:T(1,128)S(1)}, f32[1,27,2048]{2,0,1:T(1,128)}, u32[]{:S(2)}) copy-start(f32[1,27,2048]{2,0,1:T(1,128)} %param.7) | copy-start | bytes 663556
  86.9 42.1 %copy-start.4 = (f32[1,27,2048]{2,0,1:T(1,128)S(1)}, f32[1,27,2048]{2,0,1:T(1,128)}, u32[]{:S(2)}) copy-start(f32[1,27,2048]{2,0,1:T(1,128)} %param.9) | copy-start | bytes 663556
  86.9 36.2 %collective-permute-start.2 = (f32[32,6,256]{2,0,1:T(8,128)S(1)}, f32[32,6,256]{2,0,1:T(8,128)S(1)}, u32[]{:S(2)}, u32[]{:S(2)}) collective-permute-start(f32[32,6,256]{2,0,1:T(8,128)S(1)} %slice_bitcast_fusion.1), channel_id=1, source_target_pairs={{1,0},{2,1},{3,2},{5,4},{6,5},{7,6},{9,8},{10,9},{11,10},{13,12},{... | collective-permute-start | bytes 589832 | tf_op jit(solution)/shard_map/ppermute | solution.py:13
  124.3 13.4 %collective-permute-start.3 = (bf16[32,6,6,256]{3,0,2,1:T(8,128)(2,1)S(1)}, bf16[32,6,6,256]{3,0,2,1:T(8,128)(2,1)S(1)}, u32[]{:S(2)}, u32[]{:S(2)}) collective-permute-start(bf16[32,6,6,256]{3,0,2,1:T(8,128)(2,1)S(1)} %pad_maximum_fusion), channel_id=1, source_target_pairs={{4,0},{8,4},{12,8},{5,1},{9,5},{13,9},{6,2},{10,6},{14,10},{7,3},{... | collective-permute-start | bytes 1769480 | tf_op jit(solution)/shard_map/ppermute | solution.py:13
